TPU v7x, 32 devices: a whole 2x2x4 slice. The times are simulated.
32 devices in a mesh: dp: 8 (over z, x), seq: 4 (over y, core).
Axes of the slice: x: 2, y: 2, z: 4, core: 2. Of those that a mesh axis runs over, the one named last changes fastest.
Arguments:
- tokens: bfloat16 [32, 6144], P('dp', 'seq'), may hold values from -6 to 6
- expert_ids: int32 [32, 2], P('dp'), may hold values from 0 to 7, all different within a row; in each aligned block of 4 rows (0 to 3, 4 to 7, ...) at most 2 rows name the same one
- router: bfloat16 [6144, 8], P('seq'), may hold values from -0.21875 to 0.21875
- w_gate: bfloat16 [5, 6144, 16384], P(None, 'seq', 'dp'), may hold values from -0.078125 to 0.078125
- w_up: bfloat16 [5, 6144, 16384], P(None, 'seq', 'dp'), may hold values from -0.078125 to 0.078125
- w_down: bfloat16 [5, 16384, 6144], P(None, 'dp', 'seq'), may hold values from -0.046875 to 0.046875
Outputs:
- mixed: bfloat16 [32, 6144], P('dp', 'seq')
Inputs may be any that keep to these rules, and one draw needn't show every extreme that they name: `expert_ids`: each row names 2 different experts. The 4 tokens of one index of dp name any expert at most 2 times, a bound that some block reaches.
All inputs are finite; a program needn't handle non-finite values.
Results may differ from a plain program's by a relative error of at most 0.0049.
Values may be sent and summed in bfloat16 or wider, within the bound.
No kernel may reach another device: no remote copies, remote signals or barrier semaphores. Data moves between devices by JAX's collectives and lax.ppermute only.
A program may use at most 192 MiB of HBM per device.

v0:
```python
import jax
import jax.numpy as jnp
from jax import lax
from jax.sharding import PartitionSpec as P

MOST = 2


def expert_rows(routes, expert, capacity):
    member = jnp.any(routes == expert, axis=1)
    position = jnp.cumsum(member.astype(jnp.int32)) - 1
    target = jnp.where(member, position, capacity)
    count_all = routes.shape[0]
    row_token = (
        jnp.zeros((capacity,), jnp.int32)
        .at[target]
        .set(jnp.arange(count_all, dtype=jnp.int32), mode="drop")
    )
    live_count = jnp.sum(member.astype(jnp.int32))
    return (row_token, jnp.maximum(position, 0), live_count)


def body(tokens, expert_ids, router, w_gate, w_up, w_down):
    gathered = lax.all_gather(tokens, "dp", axis=0, tiled=True)
    routes = lax.all_gather(expert_ids, "dp", axis=0, tiled=True)
    capacity = MOST * lax.axis_size("dp")
    block_rows = min(128, capacity)
    window_size = w_gate.shape[0]
    buffers = []
    positions = []
    live_blocks = []
    for expert in range(window_size):
        row_token, position, live_count = expert_rows(routes, expert, capacity)
        buffers.append(gathered[row_token])
        positions.append(position)
        live_blocks.append((live_count + block_rows - 1) // block_rows)
    gate_list = []
    up_list = []
    for expert in range(window_size):
        gate_part = jnp.dot(buffers[expert], w_gate[expert], preferred_element_type=jnp.float32)
        up_part = jnp.dot(buffers[expert], w_up[expert], preferred_element_type=jnp.float32)
        gate_list.append(gate_part)
        up_list.append(up_part)
    gate_parts = jnp.stack(gate_list)
    up_parts = jnp.stack(up_list)
    logit_part = jnp.dot(gathered, router, preferred_element_type=jnp.float32)
    gate_sum, up_sum, logits = lax.psum((gate_parts, up_parts, logit_part), "seq")
    hidden = (jax.nn.silu(gate_sum) * up_sum).astype(jnp.bfloat16)
    chosen = jnp.take_along_axis(logits, routes, axis=1)
    share_first = 1.0 / (1.0 + jnp.exp(chosen[:, 1] - chosen[:, 0]))
    share_second = 1.0 / (1.0 + jnp.exp(chosen[:, 0] - chosen[:, 1]))
    partial_value = jnp.zeros((gathered.shape[0], w_down.shape[2]), jnp.float32)
    for expert in range(window_size):
        expert_out = jnp.dot(hidden[expert], w_down[expert], preferred_element_type=jnp.float32)
        weighting = jnp.where(routes[:, 0] == expert, share_first, jnp.float32(0.0))
        weighting = weighting + jnp.where(routes[:, 1] == expert, share_second, jnp.float32(0.0))
        partial_value = partial_value + weighting[:, None] * expert_out[positions[expert]]
    return lax.psum_scatter(partial_value, "dp", scatter_dimension=0, tiled=True).astype(
        jnp.bfloat16
    )


def solution(mesh):
    placed = (
        P("dp", "seq"),
        P("dp", None),
        P("seq", None),
        P(None, "seq", "dp"),
        P(None, "seq", "dp"),
        P(None, "dp", "seq"),
    )
    return jax.shard_map(
        body, mesh=mesh, in_specs=placed, out_specs=P("dp", "seq"), check_vma=False
    )
```

profile of v0, /device:TPU:0, one launch (start us, length us, event | category | flops | bytes accessed | tf_op | source)
XLA Modules:
  0.0 207.5 jit_solution(11027577087069102119)
XLA Ops:
  6.5 22.7 %all-gather = s32[8,4,2]{1,2,0:T(2,128)S(1)} all-gather(s32[1,4,2]{1,2,0:T(2,128)} %bitcast.182), channel_id=1, replica_groups=mesh['dp'=8,'seq'=4] {'dp'}, dimensions={0}, use_global_device_ids=true | all-gather | bytes 288 | tf_op jit(solution)/shard_map/all_gather | solution.py:25
  30.3 0.7 scatter_custom_fusion
  31.3 0.7 scatter_custom_fusion.3
  32.3 0.7 scatter_custom_fusion.2
  33.2 0.7 scatter_custom_fusion.1
  34.2 0.7 scatter_custom_fusion.4
  34.9 30.8 %all-gather.1 = bf16[8,4,1536]{2,1,0:T(4,128)(2,1)S(1)} all-gather(bf16[1,4,1536]{2,1,0:T(4,128)(2,1)} %bitcast.176), channel_id=1, replica_groups=mesh['dp'=8,'seq'=4] {'dp'}, dimensions={0}, use_global_device_ids=true | all-gather | bytes 110592 | tf_op jit(solution)/shard_map/all_gather | solution.py:24
  68.7 3.9 %fusion.48 = f32[5,16,2048]{2,1,0:T(8,128)S(1)} fusion(bf16[16,1536]{1,0:T(8,128)(2,1)S(1)} %gather_fusion, bf16[5,1536,2048]{2,1,0:T(8,128)(2,1)} %param.9), kind=kOutput, calls=%fused_computation.62 | convolution fusion | flops 100663296 | bytes 6471680 | tf_op jit(solution)/shard_map/dot_general | solution.py:40
  72.6 4.4 %fusion.78 = f32[5,16,2048]{2,1,0:T(8,128)S(1)} fusion(bf16[16,1536]{1,0:T(8,128)(2,1)S(1)} %gather_fusion, bf16[5,1536,2048]{2,1,0:T(8,128)(2,1)} %param.10), kind=kOutput, calls=%fused_computation.72 | convolution fusion | flops 100663296 | bytes 6471680 | tf_op jit(solution)/shard_map/dot_general | solution.py:41
  77.0 4.5 %fusion.54 = f32[5,16,2048]{2,1,0:T(8,128)S(1)} fusion(f32[5,16,2048]{2,1,0:T(8,128)S(1)} %fusion.48, bf16[16,1536]{1,0:T(8,128)(2,1)S(1)} %gather_fusion.1, bf16[5,1536,2048]{2,1,0:T(8,128)(2,1)} %param.9), kind=kOutput, calls=%fused_computation.64 | convolution fusion | flops 100663296 | bytes 6471680 | tf_op jit(solution)/shard_map/dot_general | solution.py:40
  81.4 4.5 %fusion.84 = f32[5,16,2048]{2,1,0:T(8,128)S(1)} fusion(f32[5,16,2048]{2,1,0:T(8,128)S(1)} %fusion.78, bf16[16,1536]{1,0:T(8,128)(2,1)S(1)} %gather_fusion.1, bf16[5,1536,2048]{2,1,0:T(8,128)(2,1)} %param.10), kind=kOutput, calls=%fused_computation.74 | convolution fusion | flops 100663296 | bytes 6471680 | tf_op jit(solution)/shard_map/dot_general | solution.py:41
  85.9 3.7 %fusion.60 = f32[5,16,2048]{2,1,0:T(8,128)S(1)} fusion(f32[5,16,2048]{2,1,0:T(8,128)S(1)} %fusion.54, bf16[16,1536]{1,0:T(8,128)(2,1)S(1)} %gather_fusion.2, bf16[5,1536,2048]{2,1,0:T(8,128)(2,1)} %param.9), kind=kOutput, calls=%fused_computation.66 | convolution fusion | flops 100663296 | bytes 6471680 | tf_op jit(solution)/shard_map/dot_general | solution.py:40
  89.6 0.9 fusion.90
  90.6 3.7 %fusion.66 = f32[5,16,2048]{2,1,0:T(8,128)S(1)} fusion(f32[5,16,2048]{2,1,0:T(8,128)S(1)} %fusion.60, bf16[16,1536]{1,0:T(8,128)(2,1)S(1)} %gather_fusion.3, bf16[5,1536,2048]{2,1,0:T(8,128)(2,1)} %param.9), kind=kOutput, calls=%fused_computation.68 | convolution fusion | flops 100663296 | bytes 6471680 | tf_op jit(solution)/shard_map/dot_general | solution.py:40
  94.3 0.9 fusion.96
  95.2 3.7 %fusion.72 = f32[5,16,2048]{2,1,0:T(8,128)S(1)} fusion(f32[5,16,2048]{2,1,0:T(8,128)S(1)} %fusion.66, bf16[16,1536]{1,0:T(8,128)(2,1)S(1)} %gather_fusion.4, bf16[5,1536,2048]{2,1,0:T(8,128)(2,1)} %param.9), kind=kOutput, calls=%fused_computation.70 | convolution fusion | flops 100663296 | bytes 6471680 | tf_op jit(solution)/shard_map/dot_general | solution.py:40
  99.0 0.9 fusion.102
  99.9 0.9 copy-done.2
  101.2 5.7 %psum.21 = f32[32,8]{0,1:T(8,128)S(1)} all-reduce(f32[32,8]{0,1:T(8,128)S(1)} %fusion.120), channel_id=1, replica_groups=mesh['dp'=8,'seq'=4] {'seq'}, use_global_device_ids=true, to_apply=%region_0.0 | all-reduce | flops 256 | bytes 2048 | tf_op jit(solution)/shard_map/psum | solution.py:47
  106.9 0.7 gather_fusion.10
  109.4 28.0 %all-reduce.5.cloned.1.call-done = (f32[5,16,2048]{2,1,0:T(8,128)}, f32[5,16,2048]{2,1,0:T(8,128)}) async-done(((f32[5,16,2048]{2,1,0:T(8,128)}, f32[5,16,2048]{2,1,0:T(8,128)}), (f32[5,16,2048]{2,1,0:T(8,128)}, f32[5,16,2048]{2,1,0:T(8,128)})) %all-reduce.5.cloned.1.call-update) | async-done | bytes 1310736 | tf_op jit(solution)/shard_map/psum | solution.py:47
  137.4 1.5 multiply_convert_fusion
  138.9 3.7 %fusion = f32[16,1536]{1,0:T(8,128)S(1)} fusion(bf16[5,2048,1536]{2,1,0:T(8,128)(2,1)} %param.11, bf16[5,16,2048]{2,1,0:T(8,128)(2,1)S(1)} %multiply_convert_fusion), kind=kOutput, calls=%fused_computation.16 | convolution fusion | flops 100663296 | bytes 6455296 | tf_op jit(solution)/shard_map/dot_general | solution.py:54
  142.6 3.7 %fusion.2 = f32[16,1536]{1,0:T(8,128)S(1)} fusion(bf16[5,2048,1536]{2,1,0:T(8,128)(2,1)} %param.11, bf16[5,16,2048]{2,1,0:T(8,128)(2,1)S(1)} %multiply_convert_fusion), kind=kOutput, calls=%fused_computation.18 | convolution fusion | flops 100663296 | bytes 6455296 | tf_op jit(solution)/shard_map/dot_general | solution.py:54
  146.3 3.7 %fusion.4 = f32[16,1536]{1,0:T(8,128)S(1)} fusion(bf16[5,2048,1536]{2,1,0:T(8,128)(2,1)} %param.11, bf16[5,16,2048]{2,1,0:T(8,128)(2,1)S(1)} %multiply_convert_fusion), kind=kOutput, calls=%fused_computation.20 | convolution fusion | flops 100663296 | bytes 6455296 | tf_op jit(solution)/shard_map/dot_general | solution.py:54
  150.0 3.7 %fusion.6 = f32[16,1536]{1,0:T(8,128)S(1)} fusion(bf16[5,2048,1536]{2,1,0:T(8,128)(2,1)} %param.11, bf16[5,16,2048]{2,1,0:T(8,128)(2,1)S(1)} %multiply_convert_fusion), kind=kOutput, calls=%fused_computation.22 | convolution fusion | flops 100663296 | bytes 6455296 | tf_op jit(solution)/shard_map/dot_general | solution.py:54
  153.7 3.7 %fusion.8 = f32[16,1536]{1,0:T(8,128)S(1)} fusion(bf16[5,2048,1536]{2,1,0:T(8,128)(2,1)} %param.11, bf16[5,16,2048]{2,1,0:T(8,128)(2,1)S(1)} %multiply_convert_fusion), kind=kOutput, calls=%fused_computation.24 | convolution fusion | flops 100663296 | bytes 6455296 | tf_op jit(solution)/shard_map/dot_general | solution.py:54
  157.4 0.6 gather_fusion.9
  158.1 0.6 gather_fusion.8
  158.7 0.6 gather_fusion.7
  159.3 0.6 gather_fusion.5
  160.8 39.3 %all-reduce.6 = bf16[32,1536]{1,0:T(8,128)(2,1)S(1)} all-reduce(f32[32,1536]{1,0:T(8,128)S(1)} %multiply_add_fusion), channel_id=2, replica_groups=mesh['dp'=8,'seq'=4] {'dp'}, use_global_device_ids=true, to_apply=%region_18.19.clone | all-reduce | flops 49152 | bytes 294912
  (77 shorter events, 8.1 us)
Async XLA Ops:
  6.5 94.6 %copy-start = (bf16[1536,8]{0,1:T(8,128)(2,1)S(1)}, bf16[1536,8]{0,1:T(8,128)(2,1)}, u32[]{:S(2)}) copy-start(bf16[1536,8]{0,1:T(8,128)(2,1)} %param.8) | copy-start | bytes 73732
  6.5 130.9 %all-reduce.5.cloned.1.call-start = ((), (), s32[]{:S(2)}) async-start(), calls=%async_computation | async-start | bytes 2621440 | tf_op jit(solution)/shard_map/psum | solution.py:47
  68.7 20.9 %copy-start.1 = (bf16[5,1536,2048]{2,1,0:T(8,128)(2,1)S(1)}, bf16[5,1536,2048]{2,1,0:T(8,128)(2,1)}, u32[]{:S(2)}) copy-start(bf16[5,1536,2048]{2,1,0:T(8,128)(2,1)} %param.10) | copy-start | bytes 94371840
  81.4 26.3 %copy-start.4 = (u32[32]{0:T(128)S(1)}, u32[32]{0:T(128)}, u32[]{:S(2)}) copy-start(u32[32]{0:T(128)} %constant.79) | copy-start | bytes 388
  99.0 0.9 copy-start.3
  99.9 0.9 copy-start.2
Sparse Core Ops, SparseCore 0:
  100.9 36.4 all-reduce.4
where the time goes:
time: 208 us; the launch traced here: 207 us
  blocking collectives  98.3 us (47%)
  matrix products  49.9 us (24%)
  waiting for transfers between devices  28 us (13%)
  between operations  14.4 us (7%)
  local copies, waits for them, and re-layouts  13.9 us (7%)
  other arithmetic  3.05 us (1%)
    unnamed x1, blocking collectives  39.3 us
    all_gather x1, blocking collectives, body(): gathered = lax.all_gather(tokens, 'dp', axis=0, tiled=True)  30.8 us
    psum x1, waiting for transfers between devices, body(): lax.psum((gate_parts, up_parts, logit_part), 'seq')  28 us
    all_gather x1, blocking collectives, body(): routes = lax.all_gather(expert_ids, 'dp', axis=0, tiled=True)  22.7 us
    dot_general x5, matrix products, body(): jnp.dot(buffers[expert], w_gate[expert], preferred_element_type=jnp.float32)  19.5 us
    dot_general x5, matrix products, body(): jnp.dot(hidden[expert], w_down[expert], preferred_element_type=jnp.float32)  18.6 us
    dot_general x5, matrix products, body(): jnp.dot(buffers[expert], w_up[expert], preferred_element_type=jnp.float32)  11.6 us
    psum x1, blocking collectives, body(): lax.psum((gate_parts, up_parts, logit_part), 'seq')  5.66 us
  transfers between devices with their start and end apart: 1, of which 1 were waited for; matrix products, arithmetic and copies ran while one was open for 1% of the time, Pallas kernels for 0%

commit v1 on v0

--- a/solution.py
+++ b/solution.py
@@ -21,7 +21,14 @@
 
 
 def body(tokens, expert_ids, router, w_gate, w_up, w_down):
-    gathered = lax.all_gather(tokens, "dp", axis=0, tiled=True)
+    ways, here = (lax.axis_size("dp"), lax.axis_index("dp"))
+    gathered, reach = (tokens, 1)
+    while reach < ways:
+        theirs = lax.ppermute(gathered, "dp", [(d, d ^ reach) for d in range(ways)])
+        mine_first = jnp.concatenate([gathered, theirs], axis=0)
+        theirs_first = jnp.concatenate([theirs, gathered], axis=0)
+        gathered = jnp.where(here & reach == 0, mine_first, theirs_first)
+        reach = 2 * reach
     routes = lax.all_gather(expert_ids, "dp", axis=0, tiled=True)
     capacity = MOST * lax.axis_size("dp")
     block_rows = min(128, capacity)

time: 208 us -> 188 us (0.904)
  blocking collectives: 98.3 us -> 65 us
  waiting for transfers between devices: 28 us -> 36.3 us
  starting transfers between devices: 0.01 us -> 3.11 us
    all_gather x1 -> x0, blocking collectives: 30.8 us -> none  [body(): gathered = lax.all_gather(tokens, 'dp', axis=0, tiled=True)]
    ppermute x0 -> x3, waiting for transfers between devices: none -> 6.65 us  [body(): theirs = lax.ppermute(gathered, 'dp', [(d, d ^ reach) for d in range(ways)])]
    ppermute x0 -> x3, starting transfers between devices: none -> 3.11 us  [body(): theirs = lax.ppermute(gathered, 'dp', [(d, d ^ reach) for d in range(ways)])]
    all_gather x1, blocking collectives: 22.7 us -> 20.1 us  [body(): routes = lax.all_gather(expert_ids, 'dp', axis=0, tiled=True)]
  transfers between devices with their start and end apart: 1 -> 4, of which waited for: 1 -> 3; matrix products, arithmetic and copies ran while one was open for 1% -> 5% of each run, Pallas kernels for 0% -> 0%
where the time goes in v1:
time: 188 us; the launch traced here: 187 us
  blocking collectives  65 us (35%)
  matrix products  49.9 us (27%)
  waiting for transfers between devices  36.3 us (19%)
  local copies, waits for them, and re-layouts  14.5 us (8%)
  between operations  14.4 us (8%)
  other arithmetic  3.9 us (2%)
  starting transfers between devices  3.11 us (2%)
    unnamed x1, blocking collectives  39.3 us
    psum x1, waiting for transfers between devices, body(): lax.psum((gate_parts, up_parts, logit_part), 'seq')  29.6 us
    all_gather x1, blocking collectives, body(): routes = lax.all_gather(expert_ids, 'dp', axis=0, tiled=True)  20.1 us
    dot_general x5, matrix products, body(): jnp.dot(buffers[expert], w_gate[expert], preferred_element_type=jnp.float32)  19.5 us
    dot_general x5, matrix products, body(): jnp.dot(hidden[expert], w_down[expert], preferred_element_type=jnp.float32)  18.6 us
    dot_general x5, matrix products, body(): jnp.dot(buffers[expert], w_up[expert], preferred_element_type=jnp.float32)  11.6 us
    ppermute x3, waiting for transfers between devices, body(): theirs = lax.ppermute(gathered, 'dp', [(d, d ^ reach) for d in range(ways)])  6.65 us
    psum x1, blocking collectives, body(): lax.psum((gate_parts, up_parts, logit_part), 'seq')  5.65 us
  transfers between devices with their start and end apart: 4, of which 3 were waited for; matrix products, arithmetic and copies ran while one was open for 5% of the time, Pallas kernels for 0%

profile of v1, /device:TPU:0, one launch (start us, length us, event | category | flops | bytes accessed | tf_op | source)
XLA Modules:
  0.0 187.1 jit_solution(5458492290385381992)
XLA Ops:
  6.5 3.0 %collective-permute-start = (bf16[4,1536]{1,0:T(4,128)(2,1)}, bf16[4,1536]{1,0:T(4,128)(2,1)S(1)}, u32[]{:S(2)}, u32[]{:S(2)}) collective-permute-start(bf16[4,1536]{1,0:T(4,128)(2,1)} %param.6), channel_id=1, source_target_pairs={{0,4},{4,0},{8,12},{12,8},{16,20},{20,16},{24,28},{28,24},{1,5},{5... | collective-permute-start | bytes 36872 | tf_op jit(solution)/shard_map/ppermute | solution.py:27
  9.5 20.1 %all-gather = s32[8,4,2]{1,2,0:T(2,128)S(1)} all-gather(s32[1,4,2]{1,2,0:T(2,128)} %bitcast.180), channel_id=1, replica_groups=mesh['dp'=8,'seq'=4] {'dp'}, dimensions={0}, use_global_device_ids=true | all-gather | bytes 288 | tf_op jit(solution)/shard_map/all_gather | solution.py:32
  30.8 0.7 scatter_custom_fusion
  31.7 0.7 scatter_custom_fusion.3
  32.7 0.7 scatter_custom_fusion.2
  33.7 0.7 scatter_custom_fusion.1
  34.6 0.7 scatter_custom_fusion.4
  35.5 0.8 maximum_select_fusion.2
  36.4 3.8 %collective-permute-done.1 = bf16[8,1536]{1,0:T(8,128)(2,1)S(1)} collective-permute-done((bf16[8,1536]{1,0:T(8,128)(2,1)S(1)}, bf16[8,1536]{1,0:T(8,128)(2,1)S(1)}, u32[]{:S(2)}, u32[]{:S(2)}) %collective-permute-start.1) | collective-permute-done | bytes 24608 | tf_op jit(solution)/shard_map/ppermute | solution.py:27
  40.5 1.2 dynamic-slice
  42.4 2.9 %collective-permute-done.2 = bf16[16,1536]{1,0:T(8,128)(2,1)S(1)} collective-permute-done((bf16[16,1536]{1,0:T(8,128)(2,1)S(1)}, bf16[16,1536]{1,0:T(8,128)(2,1)S(1)}, u32[]{:S(2)}, u32[]{:S(2)}) %collective-permute-start.2) | collective-permute-done | bytes 49184 | tf_op jit(solution)/shard_map/ppermute | solution.py:27
  48.3 3.9 %fusion.48 = f32[5,16,2048]{2,1,0:T(8,128)S(1)} fusion(bf16[16,1536]{1,0:T(8,128)(2,1)S(1)} %gather_fusion, bf16[5,1536,2048]{2,1,0:T(8,128)(2,1)} %param.9), kind=kOutput, calls=%fused_computation.62 | convolution fusion | flops 100663296 | bytes 6471680 | tf_op jit(solution)/shard_map/dot_general | solution.py:47
  52.1 4.4 %fusion.78 = f32[5,16,2048]{2,1,0:T(8,128)S(1)} fusion(bf16[16,1536]{1,0:T(8,128)(2,1)S(1)} %gather_fusion, bf16[5,1536,2048]{2,1,0:T(8,128)(2,1)} %param.10), kind=kOutput, calls=%fused_computation.72 | convolution fusion | flops 100663296 | bytes 6471680 | tf_op jit(solution)/shard_map/dot_general | solution.py:48
  56.5 4.5 %fusion.54 = f32[5,16,2048]{2,1,0:T(8,128)S(1)} fusion(f32[5,16,2048]{2,1,0:T(8,128)S(1)} %fusion.48, bf16[16,1536]{1,0:T(8,128)(2,1)S(1)} %gather_fusion.1, bf16[5,1536,2048]{2,1,0:T(8,128)(2,1)} %param.9), kind=kOutput, calls=%fused_computation.64 | convolution fusion | flops 100663296 | bytes 6471680 | tf_op jit(solution)/shard_map/dot_general | solution.py:47
  61.0 4.5 %fusion.84 = f32[5,16,2048]{2,1,0:T(8,128)S(1)} fusion(f32[5,16,2048]{2,1,0:T(8,128)S(1)} %fusion.78, bf16[16,1536]{1,0:T(8,128)(2,1)S(1)} %gather_fusion.1, bf16[5,1536,2048]{2,1,0:T(8,128)(2,1)} %param.10), kind=kOutput, calls=%fused_computation.74 | convolution fusion | flops 100663296 | bytes 6471680 | tf_op jit(solution)/shard_map/dot_general | solution.py:48
  65.5 3.7 %fusion.60 = f32[5,16,2048]{2,1,0:T(8,128)S(1)} fusion(f32[5,16,2048]{2,1,0:T(8,128)S(1)} %fusion.54, bf16[16,1536]{1,0:T(8,128)(2,1)S(1)} %gather_fusion.2, bf16[5,1536,2048]{2,1,0:T(8,128)(2,1)} %param.9), kind=kOutput, calls=%fused_computation.66 | convolution fusion | flops 100663296 | bytes 6471680 | tf_op jit(solution)/shard_map/dot_general | solution.py:47
  69.2 0.9 fusion.90
  70.1 3.7 %fusion.66 = f32[5,16,2048]{2,1,0:T(8,128)S(1)} fusion(f32[5,16,2048]{2,1,0:T(8,128)S(1)} %fusion.60, bf16[16,1536]{1,0:T(8,128)(2,1)S(1)} %gather_fusion.3, bf16[5,1536,2048]{2,1,0:T(8,128)(2,1)} %param.9), kind=kOutput, calls=%fused_computation.68 | convolution fusion | flops 100663296 | bytes 6471680 | tf_op jit(solution)/shard_map/dot_general | solution.py:47
  73.9 0.9 fusion.96
  74.8 3.7 %fusion.72 = f32[5,16,2048]{2,1,0:T(8,128)S(1)} fusion(f32[5,16,2048]{2,1,0:T(8,128)S(1)} %fusion.66, bf16[16,1536]{1,0:T(8,128)(2,1)S(1)} %gather_fusion.4, bf16[5,1536,2048]{2,1,0:T(8,128)(2,1)} %param.9), kind=kOutput, calls=%fused_computation.70 | convolution fusion | flops 100663296 | bytes 6471680 | tf_op jit(solution)/shard_map/dot_general | solution.py:47
  78.5 0.9 fusion.102
  79.5 0.9 copy-done.2
  80.5 5.6 %psum.21 = f32[32,8]{0,1:T(8,128)S(1)} all-reduce(f32[32,8]{0,1:T(8,128)S(1)} %fusion.120), channel_id=1, replica_groups=mesh['dp'=8,'seq'=4] {'seq'}, use_global_device_ids=true, to_apply=%region_0.1 | all-reduce | flops 256 | bytes 2048 | tf_op jit(solution)/shard_map/psum | solution.py:54
  86.1 0.7 gather_fusion.10
  87.3 29.6 %all-reduce.5.cloned.1.call-done = (f32[5,16,2048]{2,1,0:T(8,128)}, f32[5,16,2048]{2,1,0:T(8,128)}) async-done(((f32[5,16,2048]{2,1,0:T(8,128)}, f32[5,16,2048]{2,1,0:T(8,128)}), (f32[5,16,2048]{2,1,0:T(8,128)}, f32[5,16,2048]{2,1,0:T(8,128)})) %all-reduce.5.cloned.1.call-update) | async-done | bytes 1310736 | tf_op jit(solution)/shard_map/psum | solution.py:54
  117.0 1.5 multiply_convert_fusion
  118.4 3.7 %fusion = f32[16,1536]{1,0:T(8,128)S(1)} fusion(bf16[5,2048,1536]{2,1,0:T(8,128)(2,1)} %param.11, bf16[5,16,2048]{2,1,0:T(8,128)(2,1)S(1)} %multiply_convert_fusion), kind=kOutput, calls=%fused_computation.16 | convolution fusion | flops 100663296 | bytes 6455296 | tf_op jit(solution)/shard_map/dot_general | solution.py:61
  122.1 3.7 %fusion.2 = f32[16,1536]{1,0:T(8,128)S(1)} fusion(bf16[5,2048,1536]{2,1,0:T(8,128)(2,1)} %param.11, bf16[5,16,2048]{2,1,0:T(8,128)(2,1)S(1)} %multiply_convert_fusion), kind=kOutput, calls=%fused_computation.18 | convolution fusion | flops 100663296 | bytes 6455296 | tf_op jit(solution)/shard_map/dot_general | solution.py:61
  125.8 3.7 %fusion.4 = f32[16,1536]{1,0:T(8,128)S(1)} fusion(bf16[5,2048,1536]{2,1,0:T(8,128)(2,1)} %param.11, bf16[5,16,2048]{2,1,0:T(8,128)(2,1)S(1)} %multiply_convert_fusion), kind=kOutput, calls=%fused_computation.20 | convolution fusion | flops 100663296 | bytes 6455296 | tf_op jit(solution)/shard_map/dot_general | solution.py:61
  129.6 3.7 %fusion.6 = f32[16,1536]{1,0:T(8,128)S(1)} fusion(bf16[5,2048,1536]{2,1,0:T(8,128)(2,1)} %param.11, bf16[5,16,2048]{2,1,0:T(8,128)(2,1)S(1)} %multiply_convert_fusion), kind=kOutput, calls=%fused_computation.22 | convolution fusion | flops 100663296 | bytes 6455296 | tf_op jit(solution)/shard_map/dot_general | solution.py:61
  133.3 3.7 %fusion.8 = f32[16,1536]{1,0:T(8,128)S(1)} fusion(bf16[5,2048,1536]{2,1,0:T(8,128)(2,1)} %param.11, bf16[5,16,2048]{2,1,0:T(8,128)(2,1)S(1)} %multiply_convert_fusion), kind=kOutput, calls=%fused_computation.24 | convolution fusion | flops 100663296 | bytes 6455296 | tf_op jit(solution)/shard_map/dot_general | solution.py:61
  140.3 39.3 %all-reduce.6 = bf16[32,1536]{1,0:T(8,128)(2,1)S(1)} all-reduce(f32[32,1536]{1,0:T(8,128)S(1)} %multiply_add_fusion), channel_id=2, replica_groups=mesh['dp'=8,'seq'=4] {'dp'}, use_global_device_ids=true, to_apply=%region_18.19.clone | all-reduce | flops 49152 | bytes 294912
  (82 shorter events, 10.2 us)
Async XLA Ops:
  6.5 73.8 %copy-start = (bf16[1536,8]{0,1:T(8,128)(2,1)S(1)}, bf16[1536,8]{0,1:T(8,128)(2,1)}, u32[]{:S(2)}) copy-start(bf16[1536,8]{0,1:T(8,128)(2,1)} %param.8) | copy-start | bytes 73732
  6.5 110.4 %all-reduce.5.cloned.1.call-start = ((), (), s32[]{:S(2)}) async-start(), calls=%async_computation | async-start | bytes 2621440 | tf_op jit(solution)/shard_map/psum | solution.py:54
  6.5 28.9 %collective-permute-start = (bf16[4,1536]{1,0:T(4,128)(2,1)}, bf16[4,1536]{1,0:T(4,128)(2,1)S(1)}, u32[]{:S(2)}, u32[]{:S(2)}) collective-permute-start(bf16[4,1536]{1,0:T(4,128)(2,1)} %param.6), channel_id=1, source_target_pairs={{0,4},{4,0},{8,12},{12,8},{16,20},{20,16},{24,28},{28,24},{1,5},{5... | collective-permute-start | bytes 36872 | tf_op jit(solution)/shard_map/ppermute | solution.py:27
  36.3 3.9 %collective-permute-start.1 = (bf16[8,1536]{1,0:T(8,128)(2,1)S(1)}, bf16[8,1536]{1,0:T(8,128)(2,1)S(1)}, u32[]{:S(2)}, u32[]{:S(2)}) collective-permute-start(bf16[8,1536]{1,0:T(8,128)(2,1)S(1)} %maximum_select_fusion.2), channel_id=1, source_target_pairs={{0,8},{4,12},{8,0},{12,4},{16,24},{20,28},{24,16},{28,20},{1,9},{5... | collective-permute-start | bytes 73736 | tf_op jit(solution)/shard_map/ppermute | solution.py:27
  40.2 5.1 %collective-permute-start.2 = (bf16[16,1536]{1,0:T(8,128)(2,1)S(1)}, bf16[16,1536]{1,0:T(8,128)(2,1)S(1)}, u32[]{:S(2)}, u32[]{:S(2)}) collective-permute-start(bf16[16,1536]{1,0:T(8,128)(2,1)S(1)} %maximum_select_fusion.1), channel_id=1, source_target_pairs={{0,16},{4,20},{8,24},{12,28},{16,0},{20,4},{24,8},{28,12},{1,17},{... | collective-permute-start | bytes 147464 | tf_op jit(solution)/shard_map/ppermute | solution.py:27
  48.3 20.9 %copy-start.1 = (bf16[5,1536,2048]{2,1,0:T(8,128)(2,1)S(1)}, bf16[5,1536,2048]{2,1,0:T(8,128)(2,1)}, u32[]{:S(2)}) copy-start(bf16[5,1536,2048]{2,1,0:T(8,128)(2,1)} %param.10) | copy-start | bytes 94371840
  78.5 0.9 copy-start.3
  79.5 0.9 copy-start.2
Sparse Core Ops, SparseCore 0:
  80.5 36.4 all-reduce.4
